TPU v7x, 128 devices: a whole 4x4x4 slice. The times are simulated.
128 devices in a mesh: pipe: 2 (over y_lo), tensor: 8 (over y_hi, x), dp: 8 (over z, core).
Axes of the slice: x: 4, y: 4 (y_hi: 2, y_lo: 2; y = y_hi * 2 + y_lo), z: 4, core: 2. Of those that a mesh axis runs over, the one named last changes fastest.
Arguments:
- section_input: bfloat16 [8192, 1024], P('dp'), may hold values from -6 to 6
- segment_ids: int32 [8192], P('dp'), may hold values from 0 to 127, never falling along the last dimension, each value on 1 to 256 neighbouring positions
- w_qkv: bfloat16 [2, 1024, 3, 1024], P('pipe', None, None, 'tensor'), may hold values from -0.1875 to 0.1875
- qv_bias: float32 [2, 2, 1024], P('pipe', None, 'tensor'), may hold values from -3 to 3
- w_out: bfloat16 [2, 1024, 1024], P('pipe', 'tensor'), may hold values from -0.75 to 0.75
- out_bias: float32 [2, 1024], P('pipe'), may hold values from -3 to 3
- w_up: bfloat16 [2, 1024, 4096], P('pipe', None, 'tensor'), may hold values from -0.1875 to 0.1875
- up_bias: float32 [2, 4096], P('pipe', 'tensor'), may hold values from -3 to 3
- w_down: bfloat16 [2, 4096, 1024], P('pipe', 'tensor'), may hold values from -0.09375 to 0.09375
- down_bias: float32 [2, 1024], P('pipe'), may hold values from -4 to 4
- norm_gains: float32 [2, 2, 1024], P('pipe'), may hold values from 0.25 to 1.75
- norm_shifts: float32 [2, 2, 1024], P('pipe'), may hold values from -2 to 2
- out_grad: bfloat16 [8192, 1024], P('dp'), may hold values from -6 to 6
Outputs:
- section_outputs: bfloat16 [2, 8192, 1024], P('pipe', 'dp')
- input_grads: bfloat16 [2, 8192, 1024], P('pipe', 'dp')
- grad_qkv: float32 [2, 1024, 3, 1024], P('pipe', None, None, 'tensor')
- grad_qv_bias: float32 [2, 2, 1024], P('pipe', None, 'tensor')
- grad_w_out: float32 [2, 1024, 1024], P('pipe', 'tensor')
- grad_out_bias: float32 [2, 1024], P('pipe')
- grad_w_up: float32 [2, 1024, 4096], P('pipe', None, 'tensor')
- grad_up_bias: float32 [2, 4096], P('pipe', 'tensor')
- grad_w_down: float32 [2, 4096, 1024], P('pipe', 'tensor')
- grad_down_bias: float32 [2, 1024], P('pipe')
- grad_gains: float32 [2, 2, 1024], P('pipe')
- grad_shifts: float32 [2, 2, 1024], P('pipe')
Inputs may be any that keep to these rules, and one draw needn't show every extreme that they name: `segment_ids`: ids never fall along the tokens; one document is 1 to 256 tokens.
All inputs are finite; a program needn't handle non-finite values.
Results may differ from a plain program's by a relative error of at most 0.035.
Values may be sent and summed in bfloat16 or wider, within the bound.
A program may use at most 128 MiB of HBM per device.

v0:
```python
import jax
import jax.numpy as jnp
from jax import lax
from jax.sharding import PartitionSpec as P

HEAD_DIM = 64
SEQ_LEN = 256
SEQ_MB = 1
NORM_EPS = 1e-05
GELU_COEF = 0.7978845608028654
CUBIC_COEF = 0.044715
MASKED_SCORE = -1e30


def passed_along(x, axis, by):
    peers = lax.axis_size(axis)
    pairs = [(i, i + by) for i in range(peers) if 0 <= i + by < peers]
    return lax.ppermute(x, axis, pairs)


def gelu_pair(pre_act):
    tanh_val = jnp.tanh(GELU_COEF * (pre_act + CUBIC_COEF * pre_act * pre_act * pre_act))
    gelu_value = 0.5 * pre_act * (1.0 + tanh_val)
    act_slope = 0.5 * (1.0 + tanh_val) + 0.5 * pre_act * (1.0 - tanh_val * tanh_val) * GELU_COEF * (
        1.0 + 3.0 * CUBIC_COEF * pre_act * pre_act
    )
    return (gelu_value, act_slope)


def layer_norm(rows_in, norm_gain, norm_shift):
    centred = rows_in - jnp.mean(rows_in, axis=-1, keepdims=True)
    inv_std = lax.rsqrt(jnp.mean(centred * centred, axis=-1, keepdims=True) + NORM_EPS)
    normed = centred * inv_std
    return (normed * norm_gain + norm_shift, normed, inv_std)


def norm_back(grad_out, normed, inv_std, norm_gain):
    scaled = grad_out * norm_gain
    return inv_std * (
        scaled
        - jnp.mean(scaled, axis=-1, keepdims=True)
        - normed * jnp.mean(scaled * normed, axis=-1, keepdims=True)
    )


def visible(seg_rows):
    length = seg_rows.shape[-1]
    position = jnp.arange(length)
    causal = position[:, None] >= position[None, :]
    same_doc = seg_rows[:, :, None] == seg_rows[:, None, :]
    return (causal[None] & same_doc)[:, None]


def scores_of(query_rows, key_rows, seg_rows):
    score_scale = query_rows.shape[-1] ** (-0.5)
    raw_scores = (
        jnp.einsum("sqhe,skhe->shqk", query_rows, key_rows, preferred_element_type=jnp.float32)
        * score_scale
    )
    return (jnp.where(visible(seg_rows), raw_scores, MASKED_SCORE), score_scale)


def attend(query_rows, key_rows, value_rows, seg_rows):
    scores, score_scale = scores_of(query_rows, key_rows, seg_rows)
    row_max = jnp.max(scores, axis=-1, keepdims=True)
    log_total = row_max + jnp.log(jnp.sum(jnp.exp(scores - row_max), axis=-1, keepdims=True))
    prob_rows = jnp.exp(scores - log_total).astype(jnp.bfloat16)
    mix_rows = jnp.einsum(
        "shqk,skhe->sqhe", prob_rows, value_rows, preferred_element_type=jnp.float32
    ).astype(jnp.bfloat16)
    return (mix_rows, log_total)


def attend_back(query_rows, key_rows, value_rows, seg_rows, log_total, grad_mix):
    scores, score_scale = scores_of(query_rows, key_rows, seg_rows)
    prob_rows = jnp.exp(scores - log_total)
    grad_prob = jnp.einsum(
        "sqhe,skhe->shqk", grad_mix, value_rows, preferred_element_type=jnp.float32
    )
    row_delta = jnp.sum(prob_rows * grad_prob, axis=-1, keepdims=True)
    grad_scores = (prob_rows * (grad_prob - row_delta) * score_scale).astype(jnp.bfloat16)
    g_query = jnp.einsum(
        "shqk,skhe->sqhe", grad_scores, key_rows, preferred_element_type=jnp.float32
    ).astype(jnp.bfloat16)
    g_key = jnp.einsum(
        "shqk,sqhe->skhe", grad_scores, query_rows, preferred_element_type=jnp.float32
    ).astype(jnp.bfloat16)
    g_value = jnp.einsum(
        "shqk,sqhe->skhe",
        prob_rows.astype(jnp.bfloat16),
        grad_mix,
        preferred_element_type=jnp.float32,
    ).astype(jnp.bfloat16)
    return (g_query, g_key, g_value)


def on_device(
    section_input,
    segment_ids,
    w_qkv,
    qv_bias,
    w_out,
    out_bias,
    w_up,
    up_bias,
    w_down,
    down_bias,
    norm_gains,
    norm_shifts,
    out_grad,
):
    section_index = lax.axis_index("pipe")
    is_first = section_index == 0
    proj_in = w_qkv[0]
    proj_out = w_out[0]
    up_proj = w_up[0]
    down_proj = w_down[0]
    out_shift = out_bias[0]
    up_shift = up_bias[0]
    down_shift = down_bias[0]
    norm_gain = norm_gains[0]
    norm_shift = norm_shifts[0]
    dmodel = proj_in.shape[0]
    columns = proj_in.shape[2]
    heads_here = columns // HEAD_DIM
    zero_row = jnp.zeros((1, columns), jnp.float32)
    qkv_shift = jnp.concatenate([qv_bias[0][0:1], zero_row, qv_bias[0][1:2]], axis=0)
    rows_mb = SEQ_MB * SEQ_LEN
    micro_count = section_input.shape[0] // rows_mb

    def combine(partial_rows):
        summed = lax.psum(partial_rows.astype(jnp.bfloat16), "tensor").astype(jnp.float32)
        return summed

    def batch_rows(source, batch_index):
        return lax.dynamic_slice_in_dim(source, batch_index * rows_mb, rows_mb, 0)

    incoming = jnp.zeros((rows_mb, dmodel), jnp.bfloat16)
    forward_outs = []
    states = []
    for tick_index in range(micro_count + 1):
        own_rows = batch_rows(section_input, min(tick_index, micro_count - 1))
        held_rows = jnp.where(is_first, own_rows, incoming)
        batch_here = jnp.clip(tick_index - section_index, 0, micro_count - 1)
        seg_rows = lax.dynamic_slice_in_dim(segment_ids, batch_here * rows_mb, rows_mb, 0).reshape(
            SEQ_MB, SEQ_LEN
        )
        residual = held_rows.astype(jnp.float32)
        first_norm, forward_normed1, forward_inv1 = layer_norm(
            residual, norm_gain[0], norm_shift[0]
        )
        forward_first_in = first_norm.astype(jnp.bfloat16)
        forward_qkv = (
            jnp.einsum("td,dgc->tgc", forward_first_in, proj_in, preferred_element_type=jnp.float32)
            + qkv_shift
        ).astype(jnp.bfloat16)
        forward_shaped = forward_qkv.reshape(SEQ_MB, SEQ_LEN, 3, heads_here, HEAD_DIM)
        mix_rows, forward_log_total = attend(
            forward_shaped[:, :, 0], forward_shaped[:, :, 1], forward_shaped[:, :, 2], seg_rows
        )
        forward_mix_flat = mix_rows.reshape(rows_mb, columns)
        middle = (
            residual
            + combine(jnp.dot(forward_mix_flat, proj_out, preferred_element_type=jnp.float32))
            + out_shift
        )
        second_norm, forward_normed2, forward_inv2 = layer_norm(middle, norm_gain[1], norm_shift[1])
        forward_second_in = second_norm.astype(jnp.bfloat16)
        pre_act = jnp.dot(forward_second_in, up_proj, preferred_element_type=jnp.float32) + up_shift
        gelu_value, forward_act_slope = gelu_pair(pre_act)
        forward_hidden = gelu_value.astype(jnp.bfloat16)
        result = (
            middle
            + combine(jnp.dot(forward_hidden, down_proj, preferred_element_type=jnp.float32))
            + down_shift
        ).astype(jnp.bfloat16)
        forward_kept_state = (
            forward_normed1,
            forward_inv1,
            forward_first_in,
            forward_qkv,
            forward_mix_flat,
            forward_log_total,
            forward_normed2,
            forward_inv2,
            forward_second_in,
            forward_act_slope,
            forward_hidden,
            seg_rows,
        )
        result, kept_state = (result, forward_kept_state)
        forward_outs.append(result)
        states.append(kept_state)
        incoming = passed_along(result, "pipe", 1)
    returning = jnp.zeros_like(incoming)
    back_outs = []
    grad_sums = None
    for tick_index in range(micro_count + 1):
        if tick_index < micro_count:
            own_grad = batch_rows(out_grad, micro_count - 1 - tick_index)
        else:
            own_grad = jnp.zeros_like(returning)
        cotangent = jnp.where(is_first, returning, own_grad)
        (
            normed1,
            inv1,
            first_in,
            qkv,
            mix_flat,
            log_total,
            normed2,
            inv2,
            second_in,
            act_slope,
            hidden,
            backward_seg_rows,
        ) = states[micro_count - tick_index]
        grad_top = cotangent.astype(jnp.float32)
        backward_g_down = jnp.einsum(
            "tf,td->fd", hidden, cotangent, preferred_element_type=jnp.float32
        )
        backward_g_down_shift = jnp.sum(grad_top, axis=0)
        g_hidden = jnp.einsum("td,fd->tf", cotangent, down_proj, preferred_element_type=jnp.float32)
        g_pre = (g_hidden * act_slope).astype(jnp.bfloat16)
        backward_g_up = jnp.einsum(
            "td,tf->df", second_in, g_pre, preferred_element_type=jnp.float32
        )
        backward_g_up_shift = jnp.sum(g_pre.astype(jnp.float32), axis=0)
        g_second = combine(
            jnp.einsum("tf,df->td", g_pre, up_proj, preferred_element_type=jnp.float32)
        )
        g_middle = grad_top + norm_back(g_second, normed2, inv2, norm_gain[1])
        g_gain2 = jnp.sum(g_second * normed2, axis=0)
        g_shift2 = jnp.sum(g_second, axis=0)
        middle_full = g_middle.astype(jnp.bfloat16)
        backward_g_proj_out = jnp.einsum(
            "tc,td->cd", mix_flat, middle_full, preferred_element_type=jnp.float32
        )
        backward_g_out_shift = jnp.sum(g_middle, axis=0)
        g_mix = jnp.einsum(
            "td,cd->tc", middle_full, proj_out, preferred_element_type=jnp.float32
        ).astype(jnp.bfloat16)
        shaped = qkv.reshape(SEQ_MB, SEQ_LEN, 3, heads_here, HEAD_DIM)
        g_query, g_key, g_value = attend_back(
            shaped[:, :, 0],
            shaped[:, :, 1],
            shaped[:, :, 2],
            backward_seg_rows,
            log_total,
            g_mix.reshape(SEQ_MB, SEQ_LEN, heads_here, HEAD_DIM),
        )
        g_qkv = jnp.stack([g_query, g_key, g_value], axis=2).reshape(rows_mb, 3, columns)
        backward_g_proj_in = jnp.einsum(
            "td,tgc->dgc", first_in, g_qkv, preferred_element_type=jnp.float32
        )
        qkv_sums = jnp.sum(g_qkv.astype(jnp.float32), axis=0)
        backward_g_qv = jnp.stack([qkv_sums[0], qkv_sums[2]], axis=0)
        g_first = combine(
            jnp.einsum("tgc,dgc->td", g_qkv, proj_in, preferred_element_type=jnp.float32)
        )
        g_gain1 = jnp.sum(g_first * normed1, axis=0)
        g_shift1 = jnp.sum(g_first, axis=0)
        g_low = (g_middle + norm_back(g_first, normed1, inv1, norm_gain[0])).astype(jnp.bfloat16)
        grads = (
            backward_g_proj_in,
            backward_g_qv,
            backward_g_proj_out,
            backward_g_out_shift,
            backward_g_up,
            backward_g_up_shift,
            backward_g_down,
            backward_g_down_shift,
            jnp.stack([g_gain1, g_gain2]),
            jnp.stack([g_shift1, g_shift2]),
        )
        g_low, grads = (g_low, grads)
        grad_sums = (
            grads
            if grad_sums is None
            else tuple((held + fresh for held, fresh in zip(grad_sums, grads)))
        )
        back_outs.append(g_low)
        returning = passed_along(g_low, "pipe", -1)
    out_list = [
        jnp.where(is_first, forward_outs[batch_index], forward_outs[batch_index + 1])
        for batch_index in range(micro_count)
    ]
    in_list = [
        jnp.where(
            is_first, back_outs[micro_count - batch_index], back_outs[micro_count - 1 - batch_index]
        )
        for batch_index in range(micro_count)
    ]
    (
        g_proj_in,
        g_qv,
        g_proj_out,
        g_out_shift,
        g_up,
        g_up_shift,
        g_down,
        g_down_shift,
        g_gains,
        g_shifts,
    ) = grad_sums
    out_full = jnp.concatenate(out_list, axis=0)
    in_full = jnp.concatenate(in_list, axis=0)
    (
        total_qkv,
        total_qv,
        total_out,
        total_up,
        total_up_shift,
        total_down,
        total_out_shift,
        total_down_shift,
        total_gains,
        total_shifts,
    ) = (
        lax.psum(g_proj_in.astype(jnp.bfloat16), "dp").astype(jnp.float32),
        lax.psum(g_qv.astype(jnp.bfloat16), "dp").astype(jnp.float32),
        lax.psum(g_proj_out.astype(jnp.bfloat16), "dp").astype(jnp.float32),
        lax.psum(g_up.astype(jnp.bfloat16), "dp").astype(jnp.float32),
        lax.psum(g_up_shift.astype(jnp.bfloat16), "dp").astype(jnp.float32),
        lax.psum(g_down.astype(jnp.bfloat16), "dp").astype(jnp.float32),
        lax.psum(g_out_shift.astype(jnp.bfloat16), "dp").astype(jnp.float32),
        lax.psum(g_down_shift.astype(jnp.bfloat16), "dp").astype(jnp.float32),
        lax.psum(g_gains.astype(jnp.bfloat16), "dp").astype(jnp.float32),
        lax.psum(g_shifts.astype(jnp.bfloat16), "dp").astype(jnp.float32),
    )
    return (
        out_full[None],
        in_full[None],
        total_qkv[None],
        total_qv[None],
        total_out[None],
        total_out_shift[None],
        total_up[None],
        total_up_shift[None],
        total_down[None],
        total_down_shift[None],
        total_gains[None],
        total_shifts[None],
    )


def solution(mesh):
    placed = (
        P("dp", None),
        P("dp"),
        P("pipe", None, None, "tensor"),
        P("pipe", None, "tensor"),
        P("pipe", "tensor", None),
        P("pipe", None),
        P("pipe", None, "tensor"),
        P("pipe", "tensor"),
        P("pipe", "tensor", None),
        P("pipe", None),
        P("pipe", None, None),
        P("pipe", None, None),
        P("dp", None),
    )
    return jax.shard_map(
        on_device,
        mesh=mesh,
        in_specs=placed,
        out_specs=(
            P("pipe", "dp", None),
            P("pipe", "dp", None),
            P("pipe", None, None, "tensor"),
            P("pipe", None, "tensor"),
            P("pipe", "tensor", None),
            P("pipe", None),
            P("pipe", None, "tensor"),
            P("pipe", "tensor"),
            P("pipe", "tensor", None),
            P("pipe", None),
            P("pipe", None, None),
            P("pipe", None, None),
        ),
        check_vma=False,
    )
```

profile of v0, /device:TPU:0, one launch (start us, length us, event | category | flops | bytes accessed | tf_op | source)
XLA Modules:
  0.0 1970.8 jit_solution(4981071526094199700)
XLA Ops:
  17.0 87.8 %all-reduce.24.cloned.1.call-done = bf16[256,1024]{1,0:T(8,128)(2,1)} async-done(((bf16[256,1024]{1,0:T(8,128)(2,1)}), bf16[256,1024]{1,0:T(8,128)(2,1)}) %all-reduce.24.cloned.1.call-update) | async-done | bytes 524304 | tf_op jit(solution)/shard_map/psum | solution.py:132
  111.8 83.5 %all-reduce.26.cloned.1.call-done = bf16[256,1024]{1,0:T(8,128)(2,1)} async-done(((bf16[256,1024]{1,0:T(8,128)(2,1)}), bf16[256,1024]{1,0:T(8,128)(2,1)}) %all-reduce.26.cloned.1.call-update) | async-done | bytes 524304 | tf_op jit(solution)/shard_map/psum | solution.py:132
  196.8 2.5 collective-permute-start
  199.5 6.5 collective-permute-done
  211.0 85.1 %all-reduce.28.cloned.1.call-done = bf16[256,1024]{1,0:T(8,128)(2,1)} async-done(((bf16[256,1024]{1,0:T(8,128)(2,1)}), bf16[256,1024]{1,0:T(8,128)(2,1)}) %all-reduce.28.cloned.1.call-update) | async-done | bytes 524304 | tf_op jit(solution)/shard_map/psum | solution.py:132
  301.6 83.4 %all-reduce.30.cloned.1.call-done = bf16[256,1024]{1,0:T(8,128)(2,1)} async-done(((bf16[256,1024]{1,0:T(8,128)(2,1)}), bf16[256,1024]{1,0:T(8,128)(2,1)}) %all-reduce.30.cloned.1.call-update) | async-done | bytes 524304 | tf_op jit(solution)/shard_map/psum | solution.py:132
  387.3 2.5 collective-permute-start.1
  390.0 6.5 collective-permute-done.1
  401.5 85.1 %all-reduce.32.cloned.1.call-done = bf16[256,1024]{1,0:T(8,128)(2,1)} async-done(((bf16[256,1024]{1,0:T(8,128)(2,1)}), bf16[256,1024]{1,0:T(8,128)(2,1)}) %all-reduce.32.cloned.1.call-update) | async-done | bytes 524304 | tf_op jit(solution)/shard_map/psum | solution.py:132
  493.3 83.4 %all-reduce.34.cloned.1.call-done = bf16[256,1024]{1,0:T(8,128)(2,1)} async-done(((bf16[256,1024]{1,0:T(8,128)(2,1)}), bf16[256,1024]{1,0:T(8,128)(2,1)}) %all-reduce.34.cloned.1.call-update) | async-done | bytes 524304 | tf_op jit(solution)/shard_map/psum | solution.py:132
  579.1 2.7 collective-permute-start.2
  581.9 6.4 collective-permute-done.2
  593.3 85.1 %all-reduce.36.cloned.1.call-done = bf16[256,1024]{1,0:T(8,128)(2,1)} async-done(((bf16[256,1024]{1,0:T(8,128)(2,1)}), bf16[256,1024]{1,0:T(8,128)(2,1)}) %all-reduce.36.cloned.1.call-update) | async-done | bytes 524304 | tf_op jit(solution)/shard_map/psum | solution.py:132
  683.9 83.5 %all-reduce.38.cloned.1.call-done = bf16[256,1024]{1,0:T(8,128)(2,1)} async-done(((bf16[256,1024]{1,0:T(8,128)(2,1)}), bf16[256,1024]{1,0:T(8,128)(2,1)}) %all-reduce.38.cloned.1.call-update) | async-done | bytes 524304 | tf_op jit(solution)/shard_map/psum | solution.py:132
  767.4 2.5 broadcast_select_fusion.5
  769.8 2.4 collective-permute-start.3
  772.3 6.5 collective-permute-done.3
  784.3 85.1 %all-reduce.40.cloned.1.call-done = bf16[256,1024]{1,0:T(8,128)(2,1)} async-done(((bf16[256,1024]{1,0:T(8,128)(2,1)}), bf16[256,1024]{1,0:T(8,128)(2,1)}) %all-reduce.40.cloned.1.call-update) | async-done | bytes 524304 | tf_op jit(solution)/shard_map/psum | solution.py:132
  872.7 2.5 convert_reduce_fusion.24
  877.3 83.4 %all-reduce.42.cloned.1.call-done = bf16[256,1024]{1,0:T(8,128)(2,1)} async-done(((bf16[256,1024]{1,0:T(8,128)(2,1)}), bf16[256,1024]{1,0:T(8,128)(2,1)}) %all-reduce.42.cloned.1.call-update) | async-done | bytes 524304 | tf_op jit(solution)/shard_map/psum | solution.py:132
  960.7 2.4 fusion.156
  963.1 2.5 fusion.397
  970.8 2.5 convolution_convert_fusion.33
  977.8 2.4 fusion.37
  980.4 83.5 %all-reduce.44.cloned.1.call-done = bf16[256,1024]{1,0:T(8,128)(2,1)} async-done(((bf16[256,1024]{1,0:T(8,128)(2,1)}), bf16[256,1024]{1,0:T(8,128)(2,1)}) %all-reduce.44.cloned.1.call-update) | async-done | bytes 524304 | tf_op jit(solution)/shard_map/psum | solution.py:132
  1071.8 7.6 collective-permute-done.4
  1083.6 3.2 fusion.314
  1088.7 78.3 %all-reduce.46.cloned.1.call-done = bf16[256,1024]{1,0:T(8,128)(2,1)} async-done(((bf16[256,1024]{1,0:T(8,128)(2,1)}), bf16[256,1024]{1,0:T(8,128)(2,1)}) %all-reduce.46.cloned.1.call-update) | async-done | bytes 524304 | tf_op jit(solution)/shard_map/psum | solution.py:132
  1167.0 2.4 fusion.158
  1169.5 2.5 fusion.396
  1175.8 2.6 convolution_convert_fusion.31
  1178.5 2.7 convolution_convert_fusion.30
  1187.7 2.5 fusion.38
  1192.6 2.7 fusion.241
  1195.3 78.5 %all-reduce.48.cloned.1.call-done = bf16[256,1024]{1,0:T(8,128)(2,1)} async-done(((bf16[256,1024]{1,0:T(8,128)(2,1)}), bf16[256,1024]{1,0:T(8,128)(2,1)}) %all-reduce.48.cloned.1.call-update) | async-done | bytes 524304 | tf_op jit(solution)/shard_map/psum | solution.py:132
  1276.0 2.8 broadcast_select_fusion
  1284.7 5.3 collective-permute-done.5
  1295.6 2.7 fusion.239
  1299.4 79.2 %all-reduce.50.cloned.1.call-done = bf16[256,1024]{1,0:T(8,128)(2,1)} async-done(((bf16[256,1024]{1,0:T(8,128)(2,1)}), bf16[256,1024]{1,0:T(8,128)(2,1)}) %all-reduce.50.cloned.1.call-update) | async-done | bytes 524304 | tf_op jit(solution)/shard_map/psum | solution.py:132
  1381.0 2.4 fusion.398
  1388.3 2.7 convolution_convert_fusion.27
  1399.1 3.0 fusion.393
  1402.1 79.1 %all-reduce.52.cloned.1.call-done = bf16[256,1024]{1,0:T(8,128)(2,1)} async-done(((bf16[256,1024]{1,0:T(8,128)(2,1)}), bf16[256,1024]{1,0:T(8,128)(2,1)}) %all-reduce.52.cloned.1.call-update) | async-done | bytes 524304 | tf_op jit(solution)/shard_map/psum | solution.py:132
  1483.4 2.8 broadcast_select_fusion.1
  1492.0 5.4 collective-permute-done.6
  1503.1 2.9 fusion.392
  1506.0 80.1 %all-reduce.54.cloned.1.call-done = bf16[256,1024]{1,0:T(8,128)(2,1)} async-done(((bf16[256,1024]{1,0:T(8,128)(2,1)}), bf16[256,1024]{1,0:T(8,128)(2,1)}) %all-reduce.54.cloned.1.call-update) | async-done | bytes 524304 | tf_op jit(solution)/shard_map/psum | solution.py:132
  1586.1 2.4 fusion.162
  1588.5 2.6 fusion.399
  1600.4 3.1 fusion.374
  1604.0 79.6 %all-reduce.56.cloned.1.call-done = bf16[256,1024]{1,0:T(8,128)(2,1)} async-done(((bf16[256,1024]{1,0:T(8,128)(2,1)}), bf16[256,1024]{1,0:T(8,128)(2,1)}) %all-reduce.56.cloned.1.call-update) | async-done | bytes 524304 | tf_op jit(solution)/shard_map/psum | solution.py:132
  1685.8 2.8 broadcast_select_fusion.2
  1692.8 7.0 collective-permute-done.7
  1702.7 5.6 fusion.166
  1709.5 2.9 fusion.35
  1712.4 73.1 %all-reduce.58.cloned.1.call-done = bf16[256,1024]{1,0:T(8,128)(2,1)} async-done(((bf16[256,1024]{1,0:T(8,128)(2,1)}), bf16[256,1024]{1,0:T(8,128)(2,1)}) %all-reduce.58.cloned.1.call-update) | async-done | bytes 524304 | tf_op jit(solution)/shard_map/psum | solution.py:132
  1785.5 2.5 fusion.164
  1788.0 2.7 fusion.400
  1804.3 3.8 fusion.36
  1808.9 77.5 %all-reduce.62.cloned.1.call-done = (bf16[256,1024]{1,0:T(8,128)(2,1)}, bf16[256,1024]{1,0:T(8,128)(2,1)}) async-done(((bf16[256,1024]{1,0:T(8,128)(2,1)}, bf16[256,1024]{1,0:T(8,128)(2,1)}), (bf16[256,1024]{1,0:T(8,128)(2,1)}, bf16[256,1024]{1,0:T(8,128)(2,1)})) %all-reduce.62.cloned.1.call-update) | async-done | bytes 1048592 | tf_op jit(solution)/shard_map/psum | solution.py:132
  1888.5 24.1 %all-reduce = (bf16[1,2,128]{2,1,0:T(2,128)(2,1)S(1)}, bf16[1,1024]{1,0:T(2,128)(2,1)S(1)}, bf16[1,512]{1,0:T(2,128)(2,1)S(1)}, bf16[1,1024]{1,0:T(2,128)(2,1)S(...) all-reduce(bf16[1,2,128]{2,1,0:T(2,128)(2,1)S(1)} %fusion.354, ...), channel_id=1, replica_groups=mesh['pipe'=2,'tensor'=8,'dp'=8] {'dp'}, use_global_device_ids=true, to_apply=%region_81.82 | all-reduce | flops 6912 | bytes 27648 | tf_op jit(solution)/shard_map/psum | solution.py:321
  1916.2 2.6 fusion.232
  1922.3 34.8 %all-reduce.60.cloned.1.call-done = (bf16[1,1024,3,128]{3,1,2,0:T(8,128)(2,1)}, bf16[1,128,1024]{2,1,0:T(8,128)(2,1)}, bf16[1,1024,512]{2,1,0:T(8,128)(2,1)}, bf16[1,512,1024]{2,1,0:T(8,128)(2,1)}) async-done(((bf16[1,1024,3,128]{3,1,2,0:T(8,128)(2,1)}, bf16[1,128,1024]{2,1,0:T(8,128)(2,1)}, bf16[1,1024,512]{2,1,0:T(8,128)(2,1)}, bf16[1,512,1024]{2,1,0:T(8,128)(2,1)}), (bf16[1,1024,3,128]{3,1,2,0:T(8,128)(2,1)}, ...) | async-done | bytes 3145744 | tf_op jit(solution)/shard_map/psum | solution.py:320
  1957.1 2.9 broadcast_in_dim.243
  (664 shorter events, 192.9 us)
Async XLA Ops:
  7.2 103.2 %copy-start = (bf16[1,512,1024]{2,1,0:T(8,128)(2,1)S(1)}, bf16[1,512,1024]{2,1,0:T(8,128)(2,1)}, u32[]{:S(2)}) copy-start(bf16[1,512,1024]{2,1,0:T(8,128)(2,1)} %param.21) | copy-start | bytes 3145732
  7.2 97.6 %all-reduce.24.cloned.1.call-start = ((), (), s32[]{:S(2)}) async-start(), calls=%async_computation | async-start | bytes 1048576 | tf_op jit(solution)/shard_map/psum | solution.py:132
  11.5 768.9 %copy-start.146 = (f32[1,1,1024]{2,1,0:T(1,128)}, f32[1,1,1024]{2,1,0:T(1,128)S(1)}, u32[]{:S(2)}) copy-start(f32[1,1,1024]{2,1,0:T(1,128)S(1)} %get-tuple-element.104) | copy-start | bytes 12292
  15.0 89.9 %copy-start.47 = (f32[1,1024]{1,0:T(1,128)S(1)}, f32[1,1024]{1,0:T(1,128)}, u32[]{:S(2)}) copy-start(f32[1,1024]{1,0:T(1,128)} %param.18) | copy-start | bytes 12292
  15.1 91.3 %copy-start.96 = (bf16[256,3,128]{0,2,1:T(8,128)(2,1)}, bf16[256,3,128]{0,2,1:T(8,128)(2,1)S(1)}, u32[]{:S(2)}) copy-start(bf16[256,3,128]{0,2,1:T(8,128)(2,1)S(1)} %add_convert_fusion.17) | copy-start | bytes 589828
  15.5 92.5 %copy-start.2 = (bf16[1,1024,512]{2,1,0:T(8,128)(2,1)S(1)}, bf16[1,1024,512]{2,1,0:T(8,128)(2,1)}, u32[]{:S(2)}) copy-start(bf16[1,1024,512]{2,1,0:T(8,128)(2,1)} %param.19) | copy-start | bytes 3145732
  15.5 92.5 %copy-start.200 = (f32[1,512]{1,0:T(1,128)S(1)}, f32[1,512]{1,0:T(1,128)}, u32[]{:S(2)}) copy-start(f32[1,512]{1,0:T(1,128)} %param.20) | copy-start | bytes 6148
  15.5 89.3 %copy-start.130 = (f32[2,256]{1,0:T(2,128)}, f32[2,256]{1,0:T(2,128)S(1)}, u32[]{:S(2)}) copy-start(f32[2,256]{1,0:T(2,128)S(1)} %log_add_fusion.4) | copy-start | bytes 6148
  15.8 93.8 %copy-start.87 = (bf16[2,64,256]{2,1,0:T(8,128)(2,1)}, bf16[2,64,256]{2,1,0:T(8,128)(2,1)S(1)}, u32[]{:S(2)}) copy-start(bf16[2,64,256]{2,1,0:T(8,128)(2,1)S(1)} %convolution_convert_fusion.39) | copy-start | bytes 196612
  16.9 178.3 %all-reduce.26.cloned.1.call-start = ((), (), s32[]{:S(2)}) async-start(), calls=%async_computation.1 | async-start | bytes 1048576 | tf_op jit(solution)/shard_map/psum | solution.py:132
  110.4 84.8 %copy-start.116 = (f32[1,1024]{1,0:T(1,128)S(1)}, f32[1,1024]{1,0:T(1,128)}, u32[]{:S(2)}) copy-start(f32[1,1024]{1,0:T(1,128)} %param.22) | copy-start | bytes 12292
  111.7 184.3 %all-reduce.28.cloned.1.call-start = ((), (), s32[]{:S(2)}) async-start(), calls=%async_computation.2 | async-start | bytes 1048576 | tf_op jit(solution)/shard_map/psum | solution.py:132
  196.8 9.2 collective-permute-start
  209.0 87.1 %copy-start.132 = (f32[2,256]{1,0:T(2,128)}, f32[2,256]{1,0:T(2,128)S(1)}, u32[]{:S(2)}) copy-start(f32[2,256]{1,0:T(2,128)S(1)} %log_add_fusion.3) | copy-start | bytes 6148
  210.9 174.0 %all-reduce.30.cloned.1.call-start = ((), (), s32[]{:S(2)}) async-start(), calls=%async_computation.3 | async-start | bytes 1048576 | tf_op jit(solution)/shard_map/psum | solution.py:132
  300.2 84.8 %copy-start.53 = (bf16[256,1024]{1,0:T(8,128)(2,1)S(1)}, bf16[256,1024]{1,0:T(8,128)(2,1)}, u32[]{:S(2)}) copy-start(bf16[256,1024]{1,0:T(8,128)(2,1)} %copy-done.52) | copy-start | bytes 1572868
  301.5 185.1 %all-reduce.32.cloned.1.call-start = ((), (), s32[]{:S(2)}) async-start(), calls=%async_computation.4 | async-start | bytes 1048576 | tf_op jit(solution)/shard_map/psum | solution.py:132
  387.3 9.2 collective-permute-start.1
  399.5 87.2 %copy-start.134 = (f32[2,256]{1,0:T(2,128)}, f32[2,256]{1,0:T(2,128)S(1)}, u32[]{:S(2)}) copy-start(f32[2,256]{1,0:T(2,128)S(1)} %log_add_fusion.2) | copy-start | bytes 6148
  401.4 175.3 %all-reduce.34.cloned.1.call-start = ((), (), s32[]{:S(2)}) async-start(), calls=%async_computation.5 | async-start | bytes 1048576 | tf_op jit(solution)/shard_map/psum | solution.py:132
  493.3 185.0 %all-reduce.36.cloned.1.call-start = ((), (), s32[]{:S(2)}) async-start(), calls=%async_computation.6 | async-start | bytes 1048576 | tf_op jit(solution)/shard_map/psum | solution.py:132
  579.1 9.2 collective-permute-start.2
  591.2 87.1 %copy-start.135 = (f32[2,256]{1,0:T(2,128)}, f32[2,256]{1,0:T(2,128)S(1)}, u32[]{:S(2)}) copy-start(f32[2,256]{1,0:T(2,128)S(1)} %log_add_fusion.1) | copy-start | bytes 6148
  593.2 174.2 %all-reduce.38.cloned.1.call-start = ((), (), s32[]{:S(2)}) async-start(), calls=%async_computation.7 | async-start | bytes 1048576 | tf_op jit(solution)/shard_map/psum | solution.py:132
  683.8 185.6 %all-reduce.40.cloned.1.call-start = ((), (), s32[]{:S(2)}) async-start(), calls=%async_computation.8 | async-start | bytes 1048576 | tf_op jit(solution)/shard_map/psum | solution.py:132
  769.8 9.0 collective-permute-start.3
  782.3 87.1 %copy-start.136 = (f32[2,256]{1,0:T(2,128)}, f32[2,256]{1,0:T(2,128)S(1)}, u32[]{:S(2)}) copy-start(f32[2,256]{1,0:T(2,128)S(1)} %log_add_fusion) | copy-start | bytes 6148
  784.2 176.5 %all-reduce.42.cloned.1.call-start = ((), (), s32[]{:S(2)}) async-start(), calls=%async_computation.9 | async-start | bytes 1048576 | tf_op jit(solution)/shard_map/psum | solution.py:132
  870.8 92.3 %copy-start.124 = (f32[256]{0:T(256)}, f32[256]{0:T(256)S(1)}, u32[]{:S(2)}) copy-start(f32[256]{0:T(256)S(1)} %broadcast_multiply_fusion.20) | copy-start | bytes 3076
  872.2 90.9 %copy-start.144 = (f32[256]{0:T(256)}, f32[256]{0:T(256)S(1)}, u32[]{:S(2)}) copy-start(f32[256]{0:T(256)S(1)} %add_rsqrt_fusion) | copy-start | bytes 3076
  877.2 186.6 %all-reduce.44.cloned.1.call-start = ((), (), s32[]{:S(2)}) async-start(), calls=%async_computation.10 | async-start | bytes 1048576 | tf_op jit(solution)/shard_map/psum | solution.py:132
  980.3 186.7 %all-reduce.46.cloned.1.call-start = ((), (), s32[]{:S(2)}) async-start(), calls=%async_computation.11 | async-start | bytes 1048576 | tf_op jit(solution)/shard_map/psum | solution.py:132
  1068.0 11.3 collective-permute-start.4
  1083.5 190.2 %all-reduce.48.cloned.1.call-start = ((), (), s32[]{:S(2)}) async-start(), calls=%async_computation.12 | async-start | bytes 1048576 | tf_op jit(solution)/shard_map/psum | solution.py:132
  1190.2 188.5 %all-reduce.50.cloned.1.call-start = ((), (), s32[]{:S(2)}) async-start(), calls=%async_computation.13 | async-start | bytes 1048576 | tf_op jit(solution)/shard_map/psum | solution.py:132
  1278.8 11.2 collective-permute-start.5
  1295.1 186.1 %all-reduce.52.cloned.1.call-start = ((), (), s32[]{:S(2)}) async-start(), calls=%async_computation.14 | async-start | bytes 1048576 | tf_op jit(solution)/shard_map/psum | solution.py:132
  1298.4 80.3 %copy-start.19 = (bf16[256,1024]{1,0:T(8,128)(2,1)S(1)}, bf16[256,1024]{1,0:T(8,128)(2,1)}, u32[]{:S(2)}) copy-start(bf16[256,1024]{1,0:T(8,128)(2,1)} %all-reduce.32.cloned.1.call-done) | copy-start | bytes 1572868
  1298.4 80.3 %copy-start.121 = (f32[256]{0:T(256)S(1)}, f32[256]{0:T(256)}, u32[]{:S(2)}) copy-start(f32[256]{0:T(256)} %copy-done.120) | copy-start | bytes 3076
  1298.4 80.3 %copy-start.141 = (f32[256]{0:T(256)S(1)}, f32[256]{0:T(256)}, u32[]{:S(2)}) copy-start(f32[256]{0:T(256)} %copy-done.140) | copy-start | bytes 3076
  1397.7 188.4 %all-reduce.54.cloned.1.call-start = ((), (), s32[]{:S(2)}) async-start(), calls=%async_computation.15 | async-start | bytes 1048576 | tf_op jit(solution)/shard_map/psum | solution.py:132
  1486.2 11.2 collective-permute-start.6
  1502.5 181.1 %all-reduce.56.cloned.1.call-start = ((), (), s32[]{:S(2)}) async-start(), calls=%async_computation.16 | async-start | bytes 1048576 | tf_op jit(solution)/shard_map/psum | solution.py:132
  1506.0 86.0 %copy-start.10 = (bf16[1,128,1024]{2,1,0:T(8,128)(2,1)S(1)}, bf16[1,128,1024]{2,1,0:T(8,128)(2,1)}, u32[]{:S(2)}) copy-start(bf16[1,128,1024]{2,1,0:T(8,128)(2,1)} %param.17) | copy-start | bytes 786436
  1600.1 83.5 %copy-start.172 = (f32[256]{0:T(256)S(1)}, f32[256]{0:T(256)}, u32[]{:S(2)}) copy-start(f32[256]{0:T(256)} %copy-done.171) | copy-start | bytes 3076
  1600.1 83.5 %copy-start.180 = (f32[256]{0:T(256)S(1)}, f32[256]{0:T(256)}, u32[]{:S(2)}) copy-start(f32[256]{0:T(256)} %copy-done.179) | copy-start | bytes 3076
  1600.1 185.4 %all-reduce.58.cloned.1.call-start = ((), (), s32[]{:S(2)}) async-start(), calls=%async_computation.17 | async-start | bytes 1048576 | tf_op jit(solution)/shard_map/psum | solution.py:132
  1688.6 11.2 collective-permute-start.7
  1702.0 184.5 %all-reduce.62.cloned.1.call-start = ((), (), s32[]{:S(2)}) async-start(), calls=%async_computation.19 | async-start | bytes 2097152 | tf_op jit(solution)/shard_map/psum | solution.py:132
  1800.6 156.5 %all-reduce.60.cloned.1.call-start = ((), (), s32[]{:S(2)}) async-start(), calls=%async_computation.18 | async-start | bytes 6291456 | tf_op jit(solution)/shard_map/psum | solution.py:320
  1808.2 80.0 %copy-start.151 = (f32[1024]{0:T(1024)S(1)}, f32[1024]{0:T(1024)}, u32[]{:S(2)}) copy-start(f32[1024]{0:T(1024)} %get-tuple-element.43) | copy-start | bytes 12292
  1808.3 80.0 %copy-start.150 = (f32[1024]{0:T(1024)S(1)}, f32[1024]{0:T(1024)}, u32[]{:S(2)}) copy-start(f32[1024]{0:T(1024)} %get-tuple-element.16) | copy-start | bytes 12292
  1808.3 80.0 %copy-start.152 = (f32[1024]{0:T(1024)S(1)}, f32[1024]{0:T(1024)}, u32[]{:S(2)}) copy-start(f32[1024]{0:T(1024)} %get-tuple-element.24) | copy-start | bytes 12292
  1808.3 80.0 %copy-start.154 = (f32[1024]{0:T(1024)S(1)}, f32[1024]{0:T(1024)}, u32[]{:S(2)}) copy-start(f32[1024]{0:T(1024)} %get-tuple-element.18) | copy-start | bytes 12292
  1808.3 80.0 %copy-start.157 = (f32[1024]{0:T(1024)S(1)}, f32[1024]{0:T(1024)}, u32[]{:S(2)}) copy-start(f32[1024]{0:T(1024)} %get-tuple-element.26) | copy-start | bytes 12292
  1808.4 80.0 %copy-start.159 = (f32[1024]{0:T(1024)S(1)}, f32[1024]{0:T(1024)}, u32[]{:S(2)}) copy-start(f32[1024]{0:T(1024)} %get-tuple-element.20) | copy-start | bytes 12292
  1808.4 80.0 %copy-start.161 = (f32[1024]{0:T(1024)S(1)}, f32[1024]{0:T(1024)}, u32[]{:S(2)}) copy-start(f32[1024]{0:T(1024)} %get-tuple-element.28) | copy-start | bytes 12292
  1808.4 80.0 %copy-start.163 = (f32[1024]{0:T(1024)S(1)}, f32[1024]{0:T(1024)}, u32[]{:S(2)}) copy-start(f32[1024]{0:T(1024)} %get-tuple-element.22) | copy-start | bytes 12292
  1808.4 80.0 %copy-start.165 = (f32[1024]{0:T(1024)S(1)}, f32[1024]{0:T(1024)}, u32[]{:S(2)}) copy-start(f32[1024]{0:T(1024)} %get-tuple-element.30) | copy-start | bytes 12292
  1808.4 80.0 %copy-start.167 = (f32[1024]{0:T(1024)S(1)}, f32[1024]{0:T(1024)}, u32[]{:S(2)}) copy-start(f32[1024]{0:T(1024)} %get-tuple-element.12) | copy-start | bytes 12292
  1808.4 80.1 %copy-start.184 = (bf16[1,512]{1,0:T(2,128)(2,1)S(1)}, bf16[1,512]{1,0:T(2,128)(2,1)}, u32[]{:S(2)}) copy-start(bf16[1,512]{1,0:T(2,128)(2,1)} %broadcast_in_dim.244) | copy-start | bytes 3076
  1808.4 107.7 %copy-start.13 = (bf16[256,1024]{1,0:T(8,128)(2,1)S(1)}, bf16[256,1024]{1,0:T(8,128)(2,1)}, u32[]{:S(2)}) copy-start(bf16[256,1024]{1,0:T(8,128)(2,1)} %all-reduce.40.cloned.1.call-done) | copy-start | bytes 1572868
  1808.4 107.7 %copy-start.30 = (f32[256,1024]{1,0:T(8,128)S(1)}, f32[256,1024]{1,0:T(8,128)}, u32[]{:S(2)}) copy-start(f32[256,1024]{1,0:T(8,128)} %copy-done.29) | copy-start | bytes 3145732
  1808.4 107.7 %copy-start.117 = (f32[1,1024]{1,0:T(1,128)S(1)}, f32[1,1024]{1,0:T(1,128)}, u32[]{:S(2)}) copy-start(f32[1,1024]{1,0:T(1,128)} %param.22) | copy-start | bytes 12292
  (165 other events, 1192.6 us)
Sparse Core Ops, SparseCore 0:
  17.0 87.7 all-reduce.23
  111.9 83.3 all-reduce.25
  211.1 84.9 all-reduce.27
  301.6 83.3 all-reduce.29
  401.5 85.0 all-reduce.31
  493.4 83.2 all-reduce.33
  593.3 84.9 all-reduce.35
  683.9 83.3 all-reduce.37
  784.4 84.9 all-reduce.39
  877.4 83.2 all-reduce.41
  980.4 83.3 all-reduce.43
  1083.7 83.3 all-reduce.45
  1190.3 83.3 all-reduce.47
  1295.3 83.3 all-reduce.49
  1397.8 83.3 all-reduce.51
  1502.6 83.3 all-reduce.53
  1600.2 83.2 all-reduce.55
  1702.1 83.3 all-reduce.57
  1800.7 85.7 all-reduce.61
  1889.5 67.5 all-reduce.59
where the time goes:
time: 1980 us; the launch traced here: 1970 us
  waiting for transfers between devices  1640 us (83%)
  matrix products  134 us (7%)
  other arithmetic  103 us (5%)
  local copies, waits for them, and re-layouts  35.6 us (2%)
  blocking collectives  24.1 us (1%)
    psum x19, waiting for transfers between devices, combine(): lax.psum(partial_rows.astype(jnp.bfloat16), 'tensor').astype(jnp.float32)  1550 us
    ppermute x8, waiting for transfers between devices, passed_along(): return lax.ppermute(x, axis, pairs)  51.2 us
  transfers between devices with their start and end apart: 28, of which 28 were waited for; matrix products, arithmetic and copies ran while one was open for 3% of the time, Pallas kernels for 0%

commit v1 on v0

--- a/solution.py
+++ b/solution.py
@@ -129,7 +129,11 @@
     micro_count = section_input.shape[0] // rows_mb
 
     def combine(partial_rows):
-        summed = lax.psum(partial_rows.astype(jnp.bfloat16), "tensor").astype(jnp.float32)
+
+        def forms_edit(xin):
+            return jnp.sum(lax.all_gather(xin, axis_name="tensor"), 0)
+
+        summed = forms_edit(partial_rows.astype(jnp.bfloat16)).astype(jnp.float32)
         return summed
 
     def batch_rows(source, batch_index):

time: 1980 us -> 1910 us (0.965)
  waiting for transfers between devices: 1640 us -> 1510 us
  other arithmetic: 103 us -> 167 us
    psum x19 -> x0, waiting for transfers between devices: 1550 us -> none  [combine(): lax.psum(partial_rows.astype(jnp.bfloat16), 'tensor').astype(jnp.float32)]
    all_gather x0 -> x20, waiting for transfers between devices: none -> 1340 us  [forms_edit(): return jnp.sum(lax.all_gather(xin, axis_name='tensor'), 0)]
    reduce_sum x0 -> x20, other arithmetic: none -> 73.1 us  [forms_edit(): return jnp.sum(lax.all_gather(xin, axis_name='tensor'), 0)]
    ppermute x8, waiting for transfers between devices: 51.2 us -> 98.2 us  [passed_along(): return lax.ppermute(x, axis, pairs)]
    psum x1, waiting for transfers between devices: 34.8 us -> 64.2 us  [on_device(): lax.psum(g_proj_in.astype(jnp.bfloat16), 'dp').astype(jnp.float32)]
  transfers between devices with their start and end apart: 28 -> 29, of which waited for: 28 -> 29; matrix products, arithmetic and copies ran while one was open for 3% -> 3% of each run, Pallas kernels for 0% -> 0%
where the time goes in v1:
time: 1910 us; the launch traced here: 1900 us
  waiting for transfers between devices  1510 us (79%)
  other arithmetic  167 us (9%)
  matrix products  123 us (6%)
  local copies, waits for them, and re-layouts  44.9 us (2%)
  blocking collectives  25.4 us (1%)
    all_gather x20, waiting for transfers between devices, forms_edit(): return jnp.sum(lax.all_gather(xin, axis_name='tensor'), 0)  1340 us
    ppermute x8, waiting for transfers between devices, passed_along(): return lax.ppermute(x, axis, pairs)  98.2 us
    reduce_sum x20, other arithmetic, forms_edit(): return jnp.sum(lax.all_gather(xin, axis_name='tensor'), 0)  73.1 us
    psum x1, waiting for transfers between devices, on_device(): lax.psum(g_proj_in.astype(jnp.bfloat16), 'dp').astype(jnp.float32)  64.2 us
  transfers between devices with their start and end apart: 29, of which 29 were waited for; matrix products, arithmetic and copies ran while one was open for 3% of the time, Pallas kernels for 0%

profile of v1, /device:TPU:0, one launch (start us, length us, event | category | flops | bytes accessed | tf_op | source)
XLA Modules:
  0.0 1899.8 jit_solution(6527015564550638090)
XLA Ops:
  16.9 74.1 %all-gather.41.cloned.1.call-done = bf16[2048,1024]{1,0:T(8,128)(2,1)} async-done(((bf16[256,1024]{1,0:T(8,128)(2,1)}), bf16[2048,1024]{1,0:T(8,128)(2,1)}) %all-gather.41.cloned.1.call-update) | async-done | bytes 4194320 | tf_op jit(solution)/shard_map/all_gather | solution.py:134
  91.0 3.1 reduce_sum.1053
  100.2 69.5 %all-gather.43.cloned.1.call-done = bf16[2048,1024]{1,0:T(8,128)(2,1)} async-done(((bf16[256,1024]{1,0:T(8,128)(2,1)}), bf16[2048,1024]{1,0:T(8,128)(2,1)}) %all-gather.43.cloned.1.call-update) | async-done | bytes 4194320 | tf_op jit(solution)/shard_map/all_gather | solution.py:134
  169.8 3.1 reduce_sum.1056
  177.0 10.6 collective-permute-done
  192.6 71.4 %all-gather.45.cloned.1.call-done = bf16[2048,1024]{1,0:T(8,128)(2,1)} async-done(((bf16[256,1024]{1,0:T(8,128)(2,1)}), bf16[2048,1024]{1,0:T(8,128)(2,1)}) %all-gather.45.cloned.1.call-update) | async-done | bytes 4194320 | tf_op jit(solution)/shard_map/all_gather | solution.py:134
  264.0 3.1 reduce_sum.1060
  270.6 69.4 %all-gather.47.cloned.1.call-done = bf16[2048,1024]{1,0:T(8,128)(2,1)} async-done(((bf16[256,1024]{1,0:T(8,128)(2,1)}), bf16[2048,1024]{1,0:T(8,128)(2,1)}) %all-gather.47.cloned.1.call-update) | async-done | bytes 4194320 | tf_op jit(solution)/shard_map/all_gather | solution.py:134
  340.0 4.0 reduce_sum.1063
  348.8 10.7 collective-permute-done.1
  365.0 71.4 %all-gather.49.cloned.1.call-done = bf16[2048,1024]{1,0:T(8,128)(2,1)} async-done(((bf16[256,1024]{1,0:T(8,128)(2,1)}), bf16[2048,1024]{1,0:T(8,128)(2,1)}) %all-gather.49.cloned.1.call-update) | async-done | bytes 4194320 | tf_op jit(solution)/shard_map/all_gather | solution.py:134
  436.4 4.0 reduce_sum.1067
  446.0 69.6 %all-gather.51.cloned.1.call-done = bf16[2048,1024]{1,0:T(8,128)(2,1)} async-done(((bf16[256,1024]{1,0:T(8,128)(2,1)}), bf16[2048,1024]{1,0:T(8,128)(2,1)}) %all-gather.51.cloned.1.call-update) | async-done | bytes 4194320 | tf_op jit(solution)/shard_map/all_gather | solution.py:134
  515.5 3.2 reduce_sum.1070
  522.6 10.8 collective-permute-done.2
  538.8 71.3 %all-gather.53.cloned.1.call-done = bf16[2048,1024]{1,0:T(8,128)(2,1)} async-done(((bf16[256,1024]{1,0:T(8,128)(2,1)}), bf16[2048,1024]{1,0:T(8,128)(2,1)}) %all-gather.53.cloned.1.call-update) | async-done | bytes 4194320 | tf_op jit(solution)/shard_map/all_gather | solution.py:134
  610.0 3.1 reduce_sum.1074
  617.5 69.3 %all-gather.55.cloned.1.call-done = bf16[2048,1024]{1,0:T(8,128)(2,1)} async-done(((bf16[256,1024]{1,0:T(8,128)(2,1)}), bf16[2048,1024]{1,0:T(8,128)(2,1)}) %all-gather.55.cloned.1.call-update) | async-done | bytes 4194320 | tf_op jit(solution)/shard_map/all_gather | solution.py:134
  686.9 4.0 reduce_sum.1077
  695.7 10.7 collective-permute-done.3
  711.9 71.4 %all-gather.57.cloned.1.call-done = bf16[2048,1024]{1,0:T(8,128)(2,1)} async-done(((bf16[256,1024]{1,0:T(8,128)(2,1)}), bf16[2048,1024]{1,0:T(8,128)(2,1)}) %all-gather.57.cloned.1.call-update) | async-done | bytes 4194320 | tf_op jit(solution)/shard_map/all_gather | solution.py:134
  783.3 4.0 reduce_sum.1081
  795.2 69.5 %all-gather.61.cloned.1.call-done = bf16[2048,1024]{1,0:T(8,128)(2,1)} async-done(((bf16[256,1024]{1,0:T(8,128)(2,1)}), bf16[2048,1024]{1,0:T(8,128)(2,1)}) %all-gather.61.cloned.1.call-update) | async-done | bytes 4194320 | tf_op jit(solution)/shard_map/all_gather | solution.py:134
  864.8 4.0 reduce_sum.1085
  889.0 69.1 %all-gather.63.cloned.1.call-done = bf16[2048,1024]{1,0:T(8,128)(2,1)} async-done(((bf16[256,1024]{1,0:T(8,128)(2,1)}), bf16[2048,1024]{1,0:T(8,128)(2,1)}) %all-gather.63.cloned.1.call-update) | async-done | bytes 4194320 | tf_op jit(solution)/shard_map/all_gather | solution.py:134
  958.0 4.0 reduce_sum.1089
  967.6 13.9 collective-permute-done.4
  985.7 69.0 %all-gather.65.cloned.1.call-done = bf16[2048,1024]{1,0:T(8,128)(2,1)} async-done(((bf16[256,1024]{1,0:T(8,128)(2,1)}), bf16[2048,1024]{1,0:T(8,128)(2,1)}) %all-gather.65.cloned.1.call-update) | async-done | bytes 4194320 | tf_op jit(solution)/shard_map/all_gather | solution.py:134
  1054.7 4.0 reduce_sum.1092
  1067.5 2.6 convolution_convert_fusion.31
  1070.1 2.6 convolution_convert_fusion.30
  1081.8 69.6 %all-gather.67.cloned.1.call-done = bf16[2048,1024]{1,0:T(8,128)(2,1)} async-done(((bf16[256,1024]{1,0:T(8,128)(2,1)}), bf16[2048,1024]{1,0:T(8,128)(2,1)}) %all-gather.67.cloned.1.call-update) | async-done | bytes 4194320 | tf_op jit(solution)/shard_map/all_gather | solution.py:134
  1151.4 4.0 reduce_sum.1096
  1157.6 2.8 broadcast_select_fusion
  1161.7 13.9 collective-permute-done.5
  1180.8 68.8 %all-gather.69.cloned.1.call-done = bf16[2048,1024]{1,0:T(8,128)(2,1)} async-done(((bf16[256,1024]{1,0:T(8,128)(2,1)}), bf16[2048,1024]{1,0:T(8,128)(2,1)}) %all-gather.69.cloned.1.call-update) | async-done | bytes 4194320 | tf_op jit(solution)/shard_map/all_gather | solution.py:134
  1249.6 4.0 reduce_sum.1099
  1262.5 2.6 convolution_convert_fusion.28
  1265.1 2.6 convolution_convert_fusion.27
  1276.9 69.5 %all-gather.71.cloned.1.call-done = bf16[2048,1024]{1,0:T(8,128)(2,1)} async-done(((bf16[256,1024]{1,0:T(8,128)(2,1)}), bf16[2048,1024]{1,0:T(8,128)(2,1)}) %all-gather.71.cloned.1.call-update) | async-done | bytes 4194320 | tf_op jit(solution)/shard_map/all_gather | solution.py:134
  1346.5 4.0 reduce_sum.1103
  1352.7 2.8 broadcast_select_fusion.1
  1356.7 13.9 collective-permute-done.6
  1375.7 69.0 %all-gather.73.cloned.1.call-done = bf16[2048,1024]{1,0:T(8,128)(2,1)} async-done(((bf16[256,1024]{1,0:T(8,128)(2,1)}), bf16[2048,1024]{1,0:T(8,128)(2,1)}) %all-gather.73.cloned.1.call-update) | async-done | bytes 4194320 | tf_op jit(solution)/shard_map/all_gather | solution.py:134
  1444.7 4.0 reduce_sum.1106
  1457.5 2.6 convolution_convert_fusion.25
  1460.0 2.6 convolution_convert_fusion.24
  1471.8 69.6 %all-gather.75.cloned.1.call-done = bf16[2048,1024]{1,0:T(8,128)(2,1)} async-done(((bf16[256,1024]{1,0:T(8,128)(2,1)}), bf16[2048,1024]{1,0:T(8,128)(2,1)}) %all-gather.75.cloned.1.call-update) | async-done | bytes 4194320 | tf_op jit(solution)/shard_map/all_gather | solution.py:134
  1541.3 4.0 reduce_sum.1110
  1547.6 2.7 broadcast_select_fusion.2
  1551.7 13.9 collective-permute-done.7
  1571.3 3.2 fusion.314
  1576.8 2.8 fusion.241
  1595.5 2.9 fusion.35
  1598.4 39.5 %all-gather.77.cloned.1.call-done = bf16[2048,1024]{1,0:T(8,128)(2,1)} async-done(((bf16[256,1024]{1,0:T(8,128)(2,1)}), bf16[2048,1024]{1,0:T(8,128)(2,1)}) %all-gather.77.cloned.1.call-update) | async-done | bytes 4194320 | tf_op jit(solution)/shard_map/all_gather | solution.py:134
  1637.9 3.1 reduce_sum.1113
  1659.4 3.9 fusion.36
  1665.7 44.0 %all-gather.59.cloned.1.call-done = bf16[2048,1024]{1,0:T(8,128)(2,1)} async-done(((bf16[256,1024]{1,0:T(8,128)(2,1)}), bf16[2048,1024]{1,0:T(8,128)(2,1)}) %all-gather.59.cloned.1.call-update) | async-done | bytes 4194320 | tf_op jit(solution)/shard_map/all_gather | solution.py:134
  1709.7 3.2 reduce_sum.1084
  1716.6 64.2 %all-reduce.4.cloned.1.call-done = (bf16[1,1024,3,128]{3,1,2,0:T(8,128)(2,1)}, bf16[1,128,1024]{2,1,0:T(8,128)(2,1)}, bf16[1,1024,512]{2,1,0:T(8,128)(2,1)}, bf16[1,512,1024]{2,1,0:T(8,128)(2,1)}) async-done(((bf16[1,1024,3,128]{3,1,2,0:T(8,128)(2,1)}, bf16[1,128,1024]{2,1,0:T(8,128)(2,1)}, bf16[1,1024,512]{2,1,0:T(8,128)(2,1)}, bf16[1,512,1024]{2,1,0:T(8,128)(2,1)}), (bf16[1,1024,3,128]{3,1,2,0:T(8,128)(2,1)}, ...) | async-done | bytes 3145744 | tf_op jit(solution)/shard_map/psum | solution.py:324
  1780.8 2.9 broadcast_in_dim.243
  1787.4 67.7 %all-gather.79.cloned.1.call-done = bf16[2048,1024]{1,0:T(8,128)(2,1)} async-done(((bf16[256,1024]{1,0:T(8,128)(2,1)}), bf16[2048,1024]{1,0:T(8,128)(2,1)}) %all-gather.79.cloned.1.call-update) | async-done | bytes 4194320 | tf_op jit(solution)/shard_map/all_gather | solution.py:134
  1855.3 3.2 reduce_sum.1117
  1860.4 25.4 %all-reduce = (bf16[1,2,128]{2,1,0:T(2,128)(2,1)S(1)}, bf16[1,1024]{1,0:T(2,128)(2,1)S(1)}, bf16[1,512]{1,0:T(2,128)(2,1)S(1)}, bf16[1,1024]{1,0:T(2,128)(2,1)S(...) all-reduce(bf16[1,2,128]{2,1,0:T(2,128)(2,1)S(1)} %fusion.354, ...), channel_id=1, replica_groups=mesh['pipe'=2,'tensor'=8,'dp'=8] {'dp'}, use_global_device_ids=true, to_apply=%region_81.82 | all-reduce | flops 6912 | bytes 27648 | tf_op jit(solution)/shard_map/psum | solution.py:325
  (731 shorter events, 239.1 us)
Async XLA Ops:
  7.2 91.6 %copy-start = (bf16[1,512,1024]{2,1,0:T(8,128)(2,1)S(1)}, bf16[1,512,1024]{2,1,0:T(8,128)(2,1)}, u32[]{:S(2)}) copy-start(bf16[1,512,1024]{2,1,0:T(8,128)(2,1)} %param.21) | copy-start | bytes 3145732
  7.2 83.8 %all-gather.41.cloned.1.call-start = ((), (), s32[]{:S(2)}) async-start(), calls=%async_computation | async-start | bytes 4718592 | tf_op jit(solution)/shard_map/all_gather | solution.py:134
  11.5 696.5 %copy-start.166 = (f32[1,1,1024]{2,1,0:T(1,128)}, f32[1,1,1024]{2,1,0:T(1,128)S(1)}, u32[]{:S(2)}) copy-start(f32[1,1,1024]{2,1,0:T(1,128)S(1)} %get-tuple-element.102) | copy-start | bytes 12292
  15.1 79.1 %copy-start.117 = (bf16[256,3,128]{0,2,1:T(8,128)(2,1)}, bf16[256,3,128]{0,2,1:T(8,128)(2,1)S(1)}, u32[]{:S(2)}) copy-start(bf16[256,3,128]{0,2,1:T(8,128)(2,1)S(1)} %add_convert_fusion.17) | copy-start | bytes 589828
  15.4 75.6 %copy-start.34 = (f32[2,256,256]{1,2,0:T(8,128)}, f32[2,256,256]{1,2,0:T(8,128)S(1)}, u32[]{:S(2)}) copy-start(f32[2,256,256]{1,2,0:T(8,128)S(1)} %get-tuple-element.122) | copy-start | bytes 1572868
  15.5 78.6 %copy-start.151 = (f32[2,256]{1,0:T(2,128)}, f32[2,256]{1,0:T(2,128)S(1)}, u32[]{:S(2)}) copy-start(f32[2,256]{1,0:T(2,128)S(1)} %log_add_fusion.4) | copy-start | bytes 6148
  15.7 78.4 %copy-start.105 = (bf16[2,64,256]{2,1,0:T(8,128)(2,1)}, bf16[2,64,256]{2,1,0:T(8,128)(2,1)S(1)}, u32[]{:S(2)}) copy-start(bf16[2,64,256]{2,1,0:T(8,128)(2,1)S(1)} %convolution_convert_fusion.39) | copy-start | bytes 196612
  16.9 152.9 %all-gather.43.cloned.1.call-start = ((), (), s32[]{:S(2)}) async-start(), calls=%async_computation.1 | async-start | bytes 4718592 | tf_op jit(solution)/shard_map/all_gather | solution.py:134
  94.2 78.7 %copy-start.10 = (bf16[256,1024]{1,0:T(8,128)(2,1)}, bf16[256,1024]{1,0:T(8,128)(2,1)S(1)}, u32[]{:S(2)}) copy-start(bf16[256,1024]{1,0:T(8,128)(2,1)S(1)} %reduce_sum.1053) | copy-start | bytes 1572868
  98.8 70.9 %copy-start.132 = (f32[256,512]{1,0:T(8,128)}, f32[256,512]{1,0:T(8,128)S(1)}, u32[]{:S(2)}) copy-start(f32[256,512]{1,0:T(8,128)S(1)} %convolution_add_fusion.4) | copy-start | bytes 1572868
  100.2 163.9 %all-gather.45.cloned.1.call-start = ((), (), s32[]{:S(2)}) async-start(), calls=%async_computation.2 | async-start | bytes 4718592 | tf_op jit(solution)/shard_map/all_gather | solution.py:134
  172.9 16.3 copy-start.81
  174.3 15.4 copy-start.49
  174.3 13.3 collective-permute-start
  190.2 73.8 %copy-start.36 = (f32[2,256,256]{1,2,0:T(8,128)}, f32[2,256,256]{1,2,0:T(8,128)S(1)}, u32[]{:S(2)}) copy-start(f32[2,256,256]{1,2,0:T(8,128)S(1)} %get-tuple-element.124) | copy-start | bytes 1572868
  190.6 76.6 %copy-start.153 = (f32[2,256]{1,0:T(2,128)}, f32[2,256]{1,0:T(2,128)S(1)}, u32[]{:S(2)}) copy-start(f32[2,256]{1,0:T(2,128)S(1)} %log_add_fusion.3) | copy-start | bytes 6148
  192.5 147.5 %all-gather.47.cloned.1.call-start = ((), (), s32[]{:S(2)}) async-start(), calls=%async_computation.3 | async-start | bytes 4718592 | tf_op jit(solution)/shard_map/all_gather | solution.py:134
  267.1 76.9 %copy-start.12 = (bf16[256,1024]{1,0:T(8,128)(2,1)}, bf16[256,1024]{1,0:T(8,128)(2,1)S(1)}, u32[]{:S(2)}) copy-start(bf16[256,1024]{1,0:T(8,128)(2,1)S(1)} %reduce_sum.1060) | copy-start | bytes 1572868
  270.4 166.0 %all-gather.49.cloned.1.call-start = ((), (), s32[]{:S(2)}) async-start(), calls=%async_computation.4 | async-start | bytes 4718592 | tf_op jit(solution)/shard_map/all_gather | solution.py:134
  344.0 17.2 copy-start.82
  346.5 13.1 collective-permute-start.1
  363.0 77.5 %copy-start.154 = (f32[2,256]{1,0:T(2,128)}, f32[2,256]{1,0:T(2,128)S(1)}, u32[]{:S(2)}) copy-start(f32[2,256]{1,0:T(2,128)S(1)} %log_add_fusion.2) | copy-start | bytes 6148
  364.9 150.6 %all-gather.51.cloned.1.call-start = ((), (), s32[]{:S(2)}) async-start(), calls=%async_computation.5 | async-start | bytes 4718592 | tf_op jit(solution)/shard_map/all_gather | solution.py:134
  445.9 164.1 %all-gather.53.cloned.1.call-start = ((), (), s32[]{:S(2)}) async-start(), calls=%async_computation.6 | async-start | bytes 4718592 | tf_op jit(solution)/shard_map/all_gather | solution.py:134
  518.7 16.2 copy-start.83
  521.0 12.3 collective-permute-start.2
  536.7 76.4 %copy-start.155 = (f32[2,256]{1,0:T(2,128)}, f32[2,256]{1,0:T(2,128)S(1)}, u32[]{:S(2)}) copy-start(f32[2,256]{1,0:T(2,128)S(1)} %log_add_fusion.1) | copy-start | bytes 6148
  538.7 148.2 %all-gather.55.cloned.1.call-start = ((), (), s32[]{:S(2)}) async-start(), calls=%async_computation.7 | async-start | bytes 4718592 | tf_op jit(solution)/shard_map/all_gather | solution.py:134
  613.1 77.7 %copy-start.20 = (bf16[256,1024]{1,0:T(8,128)(2,1)}, bf16[256,1024]{1,0:T(8,128)(2,1)S(1)}, u32[]{:S(2)}) copy-start(bf16[256,1024]{1,0:T(8,128)(2,1)S(1)} %reduce_sum.1074) | copy-start | bytes 1572868
  617.3 166.1 %all-gather.57.cloned.1.call-start = ((), (), s32[]{:S(2)}) async-start(), calls=%async_computation.8 | async-start | bytes 4718592 | tf_op jit(solution)/shard_map/all_gather | solution.py:134
  690.9 17.2 copy-start.84
  693.4 15.3 copy-start.51
  693.4 13.1 collective-permute-start.3
  709.9 77.5 %copy-start.156 = (f32[2,256]{1,0:T(2,128)}, f32[2,256]{1,0:T(2,128)S(1)}, u32[]{:S(2)}) copy-start(f32[2,256]{1,0:T(2,128)S(1)} %log_add_fusion) | copy-start | bytes 6148
  711.8 152.9 %all-gather.61.cloned.1.call-start = ((), (), s32[]{:S(2)}) async-start(), calls=%async_computation.10 | async-start | bytes 4718592 | tf_op jit(solution)/shard_map/all_gather | solution.py:134
  788.7 82.5 %copy-start.144 = (f32[256]{0:T(256)}, f32[256]{0:T(256)S(1)}, u32[]{:S(2)}) copy-start(f32[256]{0:T(256)S(1)} %broadcast_multiply_fusion.20) | copy-start | bytes 3076
  790.1 81.1 %copy-start.164 = (f32[256]{0:T(256)}, f32[256]{0:T(256)S(1)}, u32[]{:S(2)}) copy-start(f32[256]{0:T(256)S(1)} %add_rsqrt_fusion) | copy-start | bytes 3076
  795.2 162.9 %all-gather.63.cloned.1.call-start = ((), (), s32[]{:S(2)}) async-start(), calls=%async_computation.11 | async-start | bytes 4718592 | tf_op jit(solution)/shard_map/all_gather | solution.py:134
  888.4 166.2 %all-gather.65.cloned.1.call-start = ((), (), s32[]{:S(2)}) async-start(), calls=%async_computation.12 | async-start | bytes 4718592 | tf_op jit(solution)/shard_map/all_gather | solution.py:134
  962.0 19.4 %copy-start.40 = (bf16[1024,1024]{1,0:T(8,128)(2,1)S(1)}, bf16[1024,1024]{1,0:T(8,128)(2,1)}, u32[]{:S(2)}) copy-start(bf16[1024,1024]{1,0:T(8,128)(2,1)} %param.25) | copy-start | bytes 6291460
  964.4 17.9 copy-start.129
  966.3 17.4 copy-start.48
  966.3 15.2 collective-permute-start.4
  985.7 165.7 %all-gather.67.cloned.1.call-start = ((), (), s32[]{:S(2)}) async-start(), calls=%async_computation.13 | async-start | bytes 4718592 | tf_op jit(solution)/shard_map/all_gather | solution.py:134
  1081.8 167.9 %all-gather.69.cloned.1.call-start = ((), (), s32[]{:S(2)}) async-start(), calls=%async_computation.14 | async-start | bytes 4718592 | tf_op jit(solution)/shard_map/all_gather | solution.py:134
  1157.6 19.7 %copy-start.126 = (f32[256,512]{1,0:T(8,128)S(1)}, f32[256,512]{1,0:T(8,128)}, u32[]{:S(2)}) copy-start(f32[256,512]{1,0:T(8,128)} %copy-done.125) | copy-start | bytes 1572868
  1160.4 18.2 copy-start.55
  1160.4 15.1 collective-permute-start.5
  1180.6 165.8 %all-gather.71.cloned.1.call-start = ((), (), s32[]{:S(2)}) async-start(), calls=%async_computation.15 | async-start | bytes 4718592 | tf_op jit(solution)/shard_map/all_gather | solution.py:134
  1276.9 167.8 %all-gather.73.cloned.1.call-start = ((), (), s32[]{:S(2)}) async-start(), calls=%async_computation.16 | async-start | bytes 4718592 | tf_op jit(solution)/shard_map/all_gather | solution.py:134
  1352.7 19.7 %copy-start.123 = (f32[256,512]{1,0:T(8,128)S(1)}, f32[256,512]{1,0:T(8,128)}, u32[]{:S(2)}) copy-start(f32[256,512]{1,0:T(8,128)} %copy-done.122) | copy-start | bytes 1572868
  1355.4 18.2 copy-start.56
  1355.4 15.1 collective-permute-start.6
  1375.7 165.7 %all-gather.75.cloned.1.call-start = ((), (), s32[]{:S(2)}) async-start(), calls=%async_computation.17 | async-start | bytes 4718592 | tf_op jit(solution)/shard_map/all_gather | solution.py:134
  1471.7 166.2 %all-gather.77.cloned.1.call-start = ((), (), s32[]{:S(2)}) async-start(), calls=%async_computation.18 | async-start | bytes 4718592 | tf_op jit(solution)/shard_map/all_gather | solution.py:134
  1547.6 18.0 copy-start.133
  1550.3 16.6 copy-start.53
  1550.3 17.3 copy-start.8
  1550.3 15.3 collective-permute-start.7
  1568.9 140.8 %all-gather.59.cloned.1.call-start = ((), (), s32[]{:S(2)}) async-start(), calls=%async_computation.9 | async-start | bytes 4718592 | tf_op jit(solution)/shard_map/all_gather | solution.py:134
  1576.5 204.4 %all-reduce.4.cloned.1.call-start = ((), (), s32[]{:S(2)}) async-start(), calls=%async_computation.20 | async-start | bytes 6291456 | tf_op jit(solution)/shard_map/psum | solution.py:324
  1663.3 191.8 %all-gather.79.cloned.1.call-start = ((), (), s32[]{:S(2)}) async-start(), calls=%async_computation.19 | async-start | bytes 4718592 | tf_op jit(solution)/shard_map/all_gather | solution.py:134
  1855.3 34.1 %copy-start.31 = (f32[256,1024]{1,0:T(8,128)S(1)}, f32[256,1024]{1,0:T(8,128)}, u32[]{:S(2)}) copy-start(f32[256,1024]{1,0:T(8,128)} %copy-done.30) | copy-start | bytes 3145732
  1855.3 34.1 %copy-start.54 = (bf16[256,1024]{1,0:T(8,128)(2,1)S(1)}, bf16[256,1024]{1,0:T(8,128)(2,1)}, u32[]{:S(2)}) copy-start(bf16[256,1024]{1,0:T(8,128)(2,1)} %copy-done.53) | copy-start | bytes 1572868
  (188 other events, 476.7 us)
Sparse Core Ops, SparseCore 0:
  17.0 73.9 all-gather.40
  100.3 69.4 all-gather.42
  192.6 71.3 all-gather.44
  270.5 69.4 all-gather.46
  365.1 71.3 all-gather.48
  446.0 69.4 all-gather.50
  538.8 71.1 all-gather.52
  617.4 69.4 all-gather.54
  712.0 71.3 all-gather.56
  795.3 69.4 all-gather.60
  888.6 69.4 all-gather.62
  985.8 68.8 all-gather.64
  1081.9 69.4 all-gather.66
  1180.7 68.8 all-gather.68
  1277.0 69.4 all-gather.70
  1375.8 68.8 all-gather.72
  1471.9 69.4 all-gather.74
  1569.0 68.8 all-gather.76
  1640.2 69.4 all-gather.58
  1713.3 67.4 all-reduce.3
  1783.8 71.3 all-gather.78
